TPU v7x, 32 devices: a whole 2x2x4 slice. The times are simulated.
32 devices in a mesh: gx: 4 (over y, x), gy: 2 (over core), vert: 4 (over z).
Axes of the slice: x: 2, y: 2, z: 4, core: 2. Of those that a mesh axis runs over, the one named last changes fastest.
Arguments:
- distribution: float32 [256, 64, 4096], P('gx', 'gy', 'vert'), as said below
- solid_mask: int32 [256, 64], P('gx', 'gy'), may hold values from 0 to 1, as said below
- normal_code: int32 [256, 64], P('gx', 'gy'), may hold values from 0 to 3
Outputs:
- new_field: float32 [256, 64, 4096], P('gx', 'gy', 'vert')
Inputs may be any that keep to these rules, and one draw needn't show every extreme that they name: distribution is positive. `solid_mask`: no solid cell lies in the first or last row or column of an aligned block of 64 x 32 cells.
All inputs are finite; a program needn't handle non-finite values.
Results may differ from a plain program's by a relative error of at most 0.0001.
Values sent between devices are 32-bit elements; how exact they have to be, the bound alone decides.
A program may use at most 128 MiB of HBM per device.

v0:
```python
import functools
import math

import jax
import jax.numpy as jnp
import ml_dtypes
import numpy as np
from jax import lax
from jax.experimental import pallas as pl
from jax.experimental.pallas import tpu as pltpu
from jax.sharding import PartitionSpec as P

NVEL = 16
STEPS = 3
SPAN = 12.0
COURANT = 0.08
INV_TAU = 2.0
WALL_T = 3.0
PLANE = NVEL * NVEL
LANES = 128
H = SPAN / NVEL
MESH = pl.DeviceIdType.MESH
F32 = jnp.float32
BF16 = jnp.bfloat16
HALVES = PLANE // LANES


def split3(x):
    x = np.asarray(x, np.float64)
    pieces = []
    for _ in range(3):
        piece = x.astype(np.float32).astype(ml_dtypes.bfloat16)
        pieces.append(piece)
        x = x - piece.astype(np.float64)
    return pieces


def tables(nz):
    axis = (np.arange(NVEL) - (NVEL - 1) / 2.0) * H
    vx = np.repeat(axis, NVEL)
    vy = np.tile(axis, NVEL)
    zloc = (np.arange(nz) - (nz - 1) / 2.0) * H
    lx, ly, lz = np.tile(vx, nz), np.tile(vy, nz), np.repeat(zloc, PLANE)

    def five(x, y, z):
        return [np.ones_like(x), x, y, z, x * x + y * y + z * z]

    def sides(x, y):
        return [np.maximum(x, 0), np.maximum(-x, 0), np.maximum(y, 0), np.maximum(-y, 0)]

    weight = np.zeros((40, nz * PLANE))
    for g, factor in enumerate([np.ones_like(lx)] + sides(lx, ly)):
        for r, phi in enumerate(five(lx, ly, lz)):
            weight[8 * g + r] = factor * phi
    w = np.concatenate(split3(weight), axis=0)

    norm = H**3 * (2 * math.pi * WALL_T) ** -1.5
    fx, fy, fz = np.tile(vx, NVEL), np.tile(vy, NVEL), np.repeat(axis, PLANE)
    shape = norm * np.exp(-(fx**2 + fy**2 + fz**2) / (2 * WALL_T))
    wall_norm = float(np.sum(shape * np.maximum(fx, 0)))
    wall = [
        [COURANT * float(np.sum(shape * s * phi)) for s in sides(fx, fy)]
        for phi in five(fx, fy, fz)
    ]

    cols = 2 + nz + 1 + 2
    b = np.zeros((16, cols * LANES))
    sxy = norm * np.exp(-(vx**2 + vy**2) / (2 * WALL_T))
    for half in range(2):
        ln = slice(half * LANES, (half + 1) * LANES)
        hx, hy = vx[ln], vy[ln]
        b[0, ln], b[1, ln], b[2, ln], b[3, ln] = 1.0, hx, hy, hx**2 + hy**2
        at = (3 + nz + half) * LANES
        to = slice(at, at + LANES)
        b[5 + nz, to] = COURANT * np.maximum(hx, 0) * sxy[ln]
        b[6 + nz, to] = COURANT * np.maximum(-hx, 0) * sxy[ln]
        b[7 + nz, to] = COURANT * np.maximum(hy, 0) * sxy[ln]
        b[8 + nz, to] = COURANT * np.maximum(-hy, 0) * sxy[ln]
    for z in range(nz + 1):
        b[4 + z, (2 + z) * LANES : (3 + z) * LANES] = 1.0
    bh, bm, bl = split3(b)
    bst = np.concatenate([bh, bm, bh, bl, bm, bh], axis=0)

    vec = np.zeros((8, LANES), np.float32)
    for half in range(2):
        ln = slice(half * LANES, (half + 1) * LANES)
        vec[half] = 1 - COURANT * (np.abs(vx[ln]) + np.abs(vy[ln]))
        vec[2 + half] = COURANT * np.abs(vx[ln])
    vec[4] = COURANT * np.abs(vy[:LANES])
    vec[5] = vy[:LANES] > 0
    return w, bst, vec, wall_norm, wall, norm


def lanes_of(vec):
    up = jnp.broadcast_to(vec[5:6, :], (8, LANES)) > 0.5
    sub = lax.broadcasted_iota(jnp.int32, (8, LANES), 0)
    return up, up & (sub == 0), jnp.logical_not(up) & (sub == 7)


def relax(geometry, src, dst, dst_first, pst, b_ref, vec, sz, hr, bc, halves, before, after, dot_rows):
    chunk, cols, nz, nch, sides = geometry
    cc = chunk * cols
    up, edge_lo, edge_hi = lanes_of(vec)

    def spread(k, slot):
        at = pl.ds(pl.multiple_of(k * cc, cc), cc)
        bc[slot] = lax.dot_general(pst[:, at], b_ref[...], (((0,), (0,)), ((), ())),
                                   preferred_element_type=F32)

    def rows_of(k, slot):
        for r in range(chunk):
            i = k * chunk + r

            def take(n):
                return bc[slot, r * cols : (r + 1) * cols, n * LANES : (n + 1) * LANES]

            inv_b = take(2 + nz)
            for half in range(2):
                exy = jnp.exp(take(half))
                pxy = take(3 + nz + half)
                for z in range(nz):
                    b = 2 * z + half
                    ln = slice(b * LANES, (b + 1) * LANES)
                    c = src[1 + i, :, ln]
                    side = src[i if half == 1 else i + 2, :, ln]
                    dn = pltpu.roll(c, 1, 0)
                    un = pltpu.roll(c, cols - 1, 0)
                    hrow = jnp.broadcast_to(hr[0, k, r : r + 1, ln], (8, LANES))
                    if sides == 2:
                        hrow = jnp.where(up, hrow, jnp.broadcast_to(hr[1, k, r : r + 1, ln], (8, LANES)))
                    s = []
                    for t in range(cols // 8):
                        tl = slice(8 * t, 8 * t + 8)
                        v = jnp.where(up, dn[tl], un[tl])
                        if t == 0:
                            v = jnp.where(edge_lo, hrow, v)
                        if t == cols // 8 - 1:
                            v = jnp.where(edge_hi, hrow, v)
                        s.append(v)
                    s = jnp.concatenate(s, axis=0)
                    moved = c * vec[half : half + 1, :] + side * vec[2 + half : 3 + half, :] + s * vec[4:5, :]
                    new = inv_b * (moved + pxy * sz[z]) + take(2 + z) * exy
                    dst[dst_first + i, :, ln] = new
                    if halves is not None:
                        hi = new.astype(BF16)
                        halves[slot, 0, r * cols : (r + 1) * cols, ln] = hi
                        halves[slot, 1, r * cols : (r + 1) * cols, ln] = (new - hi.astype(F32)).astype(BF16)

    spread(0, 0)

    def trip(m, carry):
        k = 2 * m
        before(k)
        spread(k + 1, 1)
        rows_of(k, 0)
        if dot_rows is not None:
            dot_rows(k, 0)
        before(k + 1)
        spread(lax.rem(k + 2, nch), 0)
        rows_of(k + 1, 1)
        if dot_rows is not None:
            dot_rows(k + 1, 1)
        after(k)
        after(k + 1)
        return carry

    lax.fori_loop(0, nch // 2, trip, 0)


def kernel(
    cfg, f_hbm, code, w_ref, b_ref, vec, f_mid, pst_out, hr_out, sz_out,
    fa, fb, bc, q, qy, qx, a_ref, r_ref, p_ref, pst, hs, hr, halves, wold, masks,
    lsem, osem, zss, zrs, xss, xrs, hss, hrs, qyss, qyrs, qxss, qxrs,
):
    rows, cols, nz, nx, ny, nv, wall_norm, wall, norm = cfg
    cells = rows * cols
    chunk = 8
    cc = chunk * cols
    nch = rows // chunk
    sides = 1 if ny == 2 else 2
    gx, gy, vt = lax.axis_index("gx"), lax.axis_index("gy"), lax.axis_index("vert")
    right, left = {"gx": lax.rem(gx + 1, nx)}, {"gx": lax.rem(gx + nx - 1, nx)}
    across = [{"gy": lax.rem(gy + 1, ny)}]
    if ny > 2:
        across.append({"gy": lax.rem(gy + ny - 1, ny)})
    peers = [{"vert": lax.rem(vt + k, nv)} for k in range(1, nv)]

    def local_copy(k):
        return pltpu.make_async_copy(
            f_hbm.at[pl.ds(k * chunk, chunk)], fa.at[pl.ds(1 + k * chunk, chunk)], lsem.at[k]
        )

    for k in range(nch):
        local_copy(k).start()

    barrier = pltpu.get_barrier_semaphore()
    everyone = [right, left] + across + peers
    for dev in everyone:
        pl.semaphore_signal(barrier, inc=1, device_id=dev, device_id_type=MESH)
    pl.semaphore_wait(barrier, len(everyone))

    def remote(src, dst, ss, rs, dev):
        return pltpu.make_async_remote_copy(
            src_ref=src, dst_ref=dst, send_sem=ss, recv_sem=rs, device_id=dev, device_id_type=MESH
        )

    def halo_x(step, src, first, dst):
        out = []
        for z in range(nz):
            hi = pl.ds((2 * z + 1) * LANES, LANES)
            lo = pl.ds(2 * z * LANES, LANES)
            out.append(remote(src.at[first + rows - 1, :, hi], dst.at[0, :, hi],
                              xss.at[step, 0, z], xrs.at[step, 0, z], right))
            out.append(remote(src.at[first, :, lo], dst.at[rows + 1, :, lo],
                              xss.at[step, 1, z], xrs.at[step, 1, z], left))
        return out

    z0 = (vt.astype(F32) * nz + (nz - 1) / 2.0 - (NVEL - 1) / 2.0) * H
    vz = [z0 + (z - (nz - 1) / 2.0) * H for z in range(nz)]
    sz = [jnp.exp(jnp.full((1, LANES), 0.0, F32) - vz[z] * vz[z] / (2 * WALL_T)) for z in range(nz)]
    up = lanes_of(vec)[0]

    def moments(hi, lo, k):
        dims = (((1,), (1,)), ((), ()))
        o = lax.dot_general(w_ref[...], hi, dims, preferred_element_type=F32)
        o = o + lax.dot_general(w_ref[...], lo, dims, preferred_element_type=F32)
        at = pl.ds(pl.multiple_of(k * cc, cc), cc)
        q[:, at] = o[0:40] + o[40:80] + o[80:120]

    def dot_rows(k, slot):
        moments(halves[slot, 0], halves[slot, 1], k)

    def mid_copy(buf, k):
        return pltpu.make_async_copy(
            buf.at[pl.ds(1 + k * chunk, chunk)], f_mid.at[pl.ds(1 + k * chunk, chunk)], osem.at[k]
        )

    def pack(step, buf, k):
        for r in range(chunk):
            i = 1 + k * chunk + r
            for b in range(2 * nz):
                ln = slice(b * LANES, (b + 1) * LANES)
                hs[step, k, r : r + 1, ln] = jnp.where(
                    up[0:1], buf[i, cols - 1 : cols, ln], buf[i, 0:1, ln]
                )

    def load_chunk(k, carry):
        local_copy(k).wait()
        x = fa[pl.ds(1 + k * chunk, chunk)].reshape(cc, nz * PLANE)
        hi = x.astype(BF16)
        moments(hi, (x - hi.astype(F32)).astype(BF16), k)
        at = pl.ds(pl.multiple_of(k * cc, cc), cc)
        ones = (lax.broadcasted_iota(jnp.int32, (8, LANES), 0) == 0).astype(BF16)
        gasb = lax.dot_general(masks[:, at].astype(BF16), ones, (((0,), (0,)), ((), ())),
                               preferred_element_type=F32)
        gasb = gasb.reshape(chunk, cols, LANES)
        for b in range(2 * nz):
            ln = slice(b * LANES, (b + 1) * LANES)
            fa[pl.ds(1 + k * chunk, chunk), :, ln] = fa[pl.ds(1 + k * chunk, chunk), :, ln] * gasb
        pack(0, fa, k)
        return carry

    flat = lax.broadcasted_iota(jnp.int32, (1, cells), 1)
    for n, on in enumerate([code[...] == 0] + [code[...] == k + 1 for k in range(4)]
                           + [code[...] > 0, flat % cols == 0, flat % cols == cols - 1]):
        masks[n : n + 1, :] = jnp.where(on, 1.0, 0.0)
    xs = halo_x(0, f_hbm, 0, fa)
    for c in xs:
        c.start()
    lax.fori_loop(0, nch, load_chunk, 0)

    first_col = masks[6:7, :] > 0.5
    last_col = masks[7:8, :] > 0.5
    gas = masks[0:1, :]
    picks = [masks[1 + k : 2 + k, :] for k in range(4)]
    solid = masks[5:6, :] > 0.5
    lane = lax.broadcasted_iota(jnp.int32, (8, cells), 1)
    row8 = lax.broadcasted_iota(jnp.int32, (8, cells), 0)

    def shift(v, s):
        return pltpu.roll(v, s % cells, 1)

    wold[...] = jnp.zeros_like(wold)
    bufs = [fa, fb]
    for step in range(STEPS):
        src, dst = bufs[step % 2], bufs[(step + 1) % 2]
        last = step == STEPS - 1
        hcopy = [remote(hs.at[step], hr.at[step, n], hss.at[step, n], hrs.at[step, n], dev)
                 for n, dev in enumerate(across)]
        qcopy = [remote(q.at[pl.ds(24, 16)], qy.at[step, n], qyss.at[step, n], qyrs.at[step, n], dev)
                 for n, dev in enumerate(across)]
        qcopy += [
            remote(q.at[pl.ds(8, 8), pl.ds(cells - LANES, LANES)], qx.at[step, 0],
                   qxss.at[step, 0], qxrs.at[step, 0], right),
            remote(q.at[pl.ds(16, 8), pl.ds(0, LANES)], qx.at[step, 1],
                   qxss.at[step, 1], qxrs.at[step, 1], left),
        ]
        for c in qcopy:
            c.start()
        for c in hcopy:
            c.start()
        if step > 0:
            xs = halo_x(step, src, 1, f_mid if last else src)
            for c in xs:
                c.start()

        xp, xm, yp, ym = (q[8 * g : 8 * g + 8, :] for g in range(1, 5))
        inc = (picks[0] * shift(xm[0:1], -cols) + picks[1] * shift(xp[0:1], cols)
               + picks[2] * shift(ym[0:1], -1) + picks[3] * shift(yp[0:1], 1))
        base = (q[0:8, :] - COURANT * (xp + xm + yp + ym)) * gas
        sxp, sxm = shift(xp * gas, cols), shift(xm * gas, -cols)
        syp, sym = shift(yp * gas, 1), shift(ym * gas, -1)
        for c in qcopy:
            c.wait()
        reps = cells // LANES
        left_in = jnp.concatenate([pltpu.roll(qx[step, 0], cols, 1)] * reps, axis=1)
        right_in = jnp.concatenate([pltpu.roll(qx[step, 1], LANES - cols, 1)] * reps, axis=1)
        sxp = jnp.where(lane < cols, left_in, sxp)
        sxm = jnp.where(lane >= cells - cols, right_in, sxm)
        syp = jnp.where(first_col, shift(qy[step, 0, 0:8], 1 - cols), syp)
        sym = jnp.where(last_col, shift(qy[step, len(across) - 1, 8:16], cols - 1), sym)
        part = base + COURANT * (sxp + sxm + syp + sym)
        z_row = part[3:4] + z0 * part[0:1]
        e_row = part[4:5] + 2 * z0 * part[3:4] + z0 * z0 * part[0:1]
        part = jnp.where(row8 == 3, z_row, jnp.where(row8 == 4, e_row, jnp.where(row8 == 5, inc, part)))
        a_ref[...] = part
        zc = [remote(a_ref.at[pl.ds(0, 6)], r_ref.at[step, k, pl.ds(0, 6)], zss.at[step, k], zrs.at[step, k], peers[k])
              for k in range(nv - 1)]
        for c in zc:
            c.start()
        for c in zc:
            c.wait()
        tot = part[0:6]
        for k in range(nv - 1):
            tot = tot + r_ref[step, k, 0:6]
        p_ref[0:6, :] = tot
        w = p_ref[5:6, :] * (1.0 / wall_norm)
        near = [shift(w, cols), shift(w, -cols), shift(w, 1), shift(w, -1)]
        mom = []
        for r in range(5):
            m = p_ref[r : r + 1, :]
            for d in range(4):
                if abs(wall[r][d]) > 1e-12 * abs(wall[0][0]):
                    m = m + wall[r][d] * near[d]
            mom.append(m)
        rho = mom[0]
        ux, uy, uz = mom[1] / rho, mom[2] / rho, mom[3] / rho
        temp = (mom[4] / rho - (ux * ux + uy * uy + uz * uz)) / 3.0
        rate = (INV_TAU / NVEL**3) * rho * jnp.exp(0.28 * jnp.log(temp))
        two_pi_t = (2.0 * math.pi) * temp
        amp = rate / (1.0 + rate) * rho * H**3 / (two_pi_t * jnp.sqrt(two_pi_t))
        inv = 1.0 / (1.0 + rate)
        ux, uy, uz = (jnp.where(solid, 0.0, v) for v in (ux, uy, uz))
        g = jnp.where(solid, 0.5 / WALL_T, 0.5 / temp)
        amp = jnp.where(solid, w * norm, amp)
        inv = jnp.where(solid, 0.0, inv)
        diff = w - wold[...]
        wold[...] = w
        lines = [-g * (ux * ux + uy * uy), 2 * g * ux, 2 * g * uy, -g]
        lines += [amp * jnp.exp(-g * (vz[z] - uz) * (vz[z] - uz)) for z in range(nz)]
        lines += [inv, shift(diff, cols), shift(diff, -cols), shift(diff, 1), shift(diff, -1)]
        lines += [jnp.zeros_like(inv)] * (16 - len(lines))
        for r in range(16):
            p_ref[r : r + 1, :] = lines[r]
        pv = p_ref[...]
        ph = pv.astype(BF16)
        rest = pv - ph.astype(F32)
        pm = rest.astype(BF16)
        plo = (rest - pm.astype(F32)).astype(BF16)
        for n, piece in enumerate([ph, ph, pm, ph, pm, plo]):
            pst[16 * n : 16 * n + 16, :] = piece

        for c in hcopy + xs:
            c.wait()
        if last:
            break

        def before(k):
            return None

        def after(k, step=step, dst=dst):
            pack(step + 1, dst, k)
            if step == STEPS - 2:
                mid_copy(dst, k).start()

        relax((chunk, cols, nz, nch, sides), src, dst, 1, pst, b_ref, vec, sz, hr.at[step],
              bc, halves, before, after, dot_rows)
    for k in range(nch):
        mid_copy(bufs[(STEPS - 1) % 2], k).wait()
    pst_out[...] = pst[...]
    hr_out[...] = hr[STEPS - 1]
    for z in range(nz):
        sz_out[z : z + 1, :] = sz[z]
    for z in range(nz, 8):
        sz_out[z : z + 1, :] = jnp.zeros((1, LANES), F32)


def finish(geometry, rows, f_mid, pst, hr, sz_ref, b_ref, vec, out_hbm, fa, fb, bc, lsem, osem):
    chunk, cols, nz, nch, sides = geometry

    def part(k):
        return pltpu.make_async_copy(
            f_mid.at[pl.ds(2 + k * chunk, chunk)], fa.at[pl.ds(2 + k * chunk, chunk)], lsem.at[k]
        )

    def out_copy(k):
        return pltpu.make_async_copy(
            fb.at[pl.ds(k * chunk, chunk)], out_hbm.at[pl.ds(k * chunk, chunk)], osem.at[k]
        )

    first = pltpu.make_async_copy(f_mid.at[pl.ds(0, 2)], fa.at[pl.ds(0, 2)], lsem.at[nch])
    first.start()
    for k in range(nch):
        part(k).start()
    first.wait()
    sz = [sz_ref[z : z + 1, :] for z in range(nz)]
    relax(geometry, fa, fb, 0, pst, b_ref, vec, sz, hr, bc, None,
          lambda k: part(k).wait(), lambda k: out_copy(k).start(), None)
    for k in range(nch):
        out_copy(k).wait()


def solution(mesh):
    nx, ny, nv = mesh.shape["gx"], mesh.shape["gy"], mesh.shape["vert"]
    sides = 1 if ny == 2 else 2

    def on_device(f, solid_mask, normal_code):
        rows, cols, vel = f.shape
        nz = vel // PLANE
        cells = rows * cols
        w, bst, vec, wall_norm, wall, norm = tables(nz)
        code = jnp.where(solid_mask == 1, normal_code + 1, 0).reshape(1, cells)
        nch = rows // 8
        geometry = (8, cols, nz, nch, sides)
        cfg = (rows, cols, nz, nx, ny, nv, wall_norm, wall, norm)
        vm = pl.BlockSpec(memory_space=pltpu.VMEM)
        hbm = pl.BlockSpec(memory_space=pl.ANY)
        dma = pltpu.SemaphoreType.DMA
        bw = bst.shape[1]
        chunk = 8
        bst, vec = jnp.asarray(bst), jnp.asarray(vec)
        f_mid, pst, hr, sz = pl.pallas_call(
            functools.partial(kernel, cfg),
            out_shape=[
                jax.ShapeDtypeStruct((rows + 2, cols, vel), F32),
                jax.ShapeDtypeStruct((96, cells), BF16),
                jax.ShapeDtypeStruct((sides, nch, chunk, vel), F32),
                jax.ShapeDtypeStruct((8, LANES), F32),
            ],
            in_specs=[hbm, vm, vm, vm, vm],
            out_specs=[pl.BlockSpec(memory_space=pltpu.HBM), vm, vm, vm],
            scratch_shapes=[
                pltpu.VMEM((rows + 2, cols, vel), F32),
                pltpu.VMEM((rows + 2, cols, vel), F32),
                pltpu.VMEM((2, chunk * cols, bw), F32),
                pltpu.VMEM((40, cells), F32),
                pltpu.VMEM((STEPS, sides, 16, cells), F32),
                pltpu.VMEM((STEPS, 2, 8, LANES), F32),
                pltpu.VMEM((8, cells), F32),
                pltpu.VMEM((STEPS, nv - 1, 8, cells), F32),
                pltpu.VMEM((16, cells), F32),
                pltpu.VMEM((96, cells), BF16),
                pltpu.VMEM((STEPS, rows // chunk, chunk, vel), F32),
                pltpu.VMEM((STEPS, sides, rows // chunk, chunk, vel), F32),
                pltpu.VMEM((2, 2, chunk * cols, vel), BF16),
                pltpu.VMEM((1, cells), F32),
                pltpu.VMEM((8, cells), F32),
                dma((rows // chunk,)), dma((rows // chunk,)),
                dma((STEPS, nv - 1)), dma((STEPS, nv - 1)),
                dma((STEPS, 2, nz)), dma((STEPS, 2, nz)),
                dma((STEPS, sides)), dma((STEPS, sides)),
                dma((STEPS, sides)), dma((STEPS, sides)),
                dma((STEPS, 2)), dma((STEPS, 2)),
            ],
            compiler_params=pltpu.CompilerParams(
                collective_id=0, has_side_effects=True, vmem_limit_bytes=60 * 2**20
            ),
        )(f, code, jnp.asarray(w), bst, vec)
        return pl.pallas_call(
            functools.partial(finish, geometry, rows),
            out_shape=jax.ShapeDtypeStruct(f.shape, F32),
            in_specs=[pl.BlockSpec(memory_space=pltpu.HBM), vm, vm, vm, vm, vm],
            out_specs=hbm,
            scratch_shapes=[
                pltpu.VMEM((rows + 2, cols, vel), F32),
                pltpu.VMEM((rows, cols, vel), F32),
                pltpu.VMEM((2, chunk * cols, bw), F32),
                dma((nch + 1,)), dma((nch,)),
            ],
            compiler_params=pltpu.CompilerParams(vmem_limit_bytes=60 * 2**20),
        )(f_mid, pst, hr, sz, bst, vec)

    placed = (P("gx", "gy", "vert"), P("gx", "gy"), P("gx", "gy"))
    return jax.shard_map(
        on_device, mesh=mesh, in_specs=placed, out_specs=P("gx", "gy", "vert"), check_vma=False
    )
```

profile of v0, /device:TPU:0, one launch (start us, length us, event | category | flops | bytes accessed | tf_op | source)
XLA Modules:
  0.0 71.3 jit_solution(2389596098839439881)
XLA Ops:
  0.0 0.7 %add_select_fusion = s32[64,32]{0,1:T(8,128)S(1)} fusion(s32[64,32]{0,1:T(8,128)} %param.8, s32[64,32]{0,1:T(8,128)} %param.7), kind=kLoop, calls=%fused_computation | loop fusion | flops 6144 | bytes 24576 | tf_op jit(solution)/shard_map/jit(_where)/select_n | solution.py:432
  0.7 0.1 copy.8
  0.8 0.7 reshape.3.code
  1.5 58.9 %shard_map.64 = (f32[66,32,1024]{2,1,0:T(8,128)}, bf16[96,2048]{1,0:T(8,128)(2,1)}, f32[1,8,8,1024]{3,2,1,0:T(8,128)}, f32[8,128]{1,0:T(8,128)}) custom-call(f32[64,32,1024]{2,1,0:T(8,128)} %f_hbm.1, s32[1,2048]{1,0:T(1,128)} %reshape.3.code, bf16[120,1024]{1,0:T(8,128)(2,1)} %constant.12.clone.w_ref, bf16[96,1152]{1,0:T(8,128)(2,1)} %constant.10.clone.b_ref, ...), custom_call_target="tpu_custom_call" | custom-call | tf_op jit(solution)/shard_map/pallas_call | solution.py:442
  60.4 10.9 %shard_map.65 = f32[64,32,1024]{2,1,0:T(8,128)} custom-call(f32[66,32,1024]{2,1,0:T(8,128)} %get-tuple-element.9.f_mid, bf16[96,2048]{1,0:T(8,128)(2,1)} %get-tuple-element.10.pst, f32[1,8,8,1024]{3,2,1,0:T(8,128)} %get-tuple-element.11.hr, f32[8,128]{1,0:T(8,128)} %get-tuple-element.12.sz_ref, bf16[96,1152]{1,0:T(8,128)(2,1)} %constant.10.clone.b_ref, ...), custom_call_target="tpu_custom_call" | custom-call | tf_op jit(solution)/shard_map/pallas_call | solution.py:479
where the time goes:
time: 71.7 us; the launch traced here: 71.3 us
  Pallas kernels  69.8 us (97%)
  local copies, waits for them, and re-layouts  0.77 us (1%)
  other arithmetic  0.74 us (1%)
    pallas_call x1, Pallas kernels, on_device(): pl.pallas_call(functools.partial(kernel, cfg), out_shape=[jax.ShapeDtypeS...  58.9 us
    pallas_call x1, Pallas kernels, on_device(): pl.pallas_call(functools.partial(finish, geometry, rows), out_shape=jax.S...  10.9 us

commit v1 on v0

v1 whole, which is shorter than its diff:
```python
import functools
import math

import jax
import jax.numpy as jnp
import ml_dtypes
import numpy as np
from jax import lax
from jax.experimental import pallas as pl
from jax.experimental.pallas import tpu as pltpu
from jax.sharding import PartitionSpec as P

NVEL = 16
STEPS = 3
SPAN = 12.0
COURANT = 0.08
INV_TAU = 2.0
WALL_T = 3.0
PLANE = NVEL * NVEL
LANES = 128
H = SPAN / NVEL
MESH = pl.DeviceIdType.MESH
F32 = jnp.float32
BF16 = jnp.bfloat16
CHUNK = 8
LAG = 2
PAD = 8
SLOTS = 16


def to_bf16(x):
    return np.asarray(x, np.float64).astype(np.float32).astype(ml_dtypes.bfloat16)


def split3(x):
    x = np.asarray(x, np.float64)
    pieces = []
    for _ in range(3):
        piece = to_bf16(x)
        pieces.append(piece)
        x = x - piece.astype(np.float64)
    return pieces


def tables(nz):
    ints = 2.0 * np.arange(NVEL) - (NVEL - 1)
    zints = 2.0 * np.arange(nz) - (nz - 1)
    kx, ky = np.repeat(ints, NVEL), np.tile(ints, NVEL)
    lx, ly, lz = np.tile(kx, nz), np.tile(ky, nz), np.repeat(zints, PLANE)
    tri = (lx * lx - 1) / 8 + (ly * ly - 1) / 8 + (lz * lz - 1) / 8

    def sides(x, y):
        return [np.maximum(x, 0), np.maximum(-x, 0), np.maximum(y, 0), np.maximum(-y, 0)]

    w = np.zeros((40, nz * PLANE), ml_dtypes.bfloat16)
    for g, s in enumerate([np.ones_like(lx)] + sides(lx, ly)):
        rows = [s, s * lx, s * ly, s * lz]
        high = to_bf16(s * tri)
        rows += [high, s * tri - high.astype(np.float64)]
        for r, row in enumerate(rows):
            w[8 * g + r] = to_bf16(row)

    axis = ints * (H / 2)
    vx, vy = np.repeat(axis, NVEL), np.tile(axis, NVEL)
    norm = H**3 * (2 * math.pi * WALL_T) ** -1.5
    fx, fy, fz = np.tile(vx, NVEL), np.tile(vy, NVEL), np.repeat(axis, PLANE)
    shape = norm * np.exp(-(fx**2 + fy**2 + fz**2) / (2 * WALL_T))
    wall_norm = float(np.sum(shape * np.maximum(fx, 0)))
    wall = [
        [COURANT * float(np.sum(shape * s * phi)) for s in sides(fx, fy)]
        for phi in [np.ones_like(fx), fx, fy, fz, fx * fx + fy * fy + fz * fz]
    ]

    cols = 2 + nz + 1 + 2
    b = np.zeros((16, cols * LANES))
    sxy = norm * np.exp(-(vx**2 + vy**2) / (2 * WALL_T))
    for half in range(2):
        ln = slice(half * LANES, (half + 1) * LANES)
        hx, hy = vx[ln], vy[ln]
        b[0, ln], b[1, ln], b[2, ln], b[3, ln] = 1.0, hx, hy, hx**2 + hy**2
        at = (3 + nz + half) * LANES
        to = slice(at, at + LANES)
        b[5 + nz, to] = COURANT * np.maximum(hx, 0) * sxy[ln]
        b[6 + nz, to] = COURANT * np.maximum(-hx, 0) * sxy[ln]
        b[7 + nz, to] = COURANT * np.maximum(hy, 0) * sxy[ln]
        b[8 + nz, to] = COURANT * np.maximum(-hy, 0) * sxy[ln]
    for z in range(nz):
        b[4 + z, (2 + z) * LANES : (3 + z) * LANES] = 1.0
    step_y = COURANT * np.abs(vy[:LANES])
    b[4 + nz, (2 + nz) * LANES : (3 + nz) * LANES] = step_y
    bh, bm, bl = split3(b)
    bst = np.concatenate([bh, bm, bh, bl, bm, bh], axis=0)

    vec = np.zeros((5, 8, LANES), np.float32)
    for half in range(2):
        ln = slice(half * LANES, (half + 1) * LANES)
        vec[half] = (1 - COURANT * (np.abs(vx[ln]) + np.abs(vy[ln]))) / step_y
        vec[2 + half] = COURANT * np.abs(vx[ln]) / step_y
    vec[4] = vy[:LANES] > 0
    return w, bst, vec, wall_norm, wall, norm


def kernel(
    cfg, f_hbm, sol, nor, w_ref, b_ref, vec, out,
    fa, fb, bc, q, qy, a_ref, r_ref, p_ref, pst, halves, wold, masks, szr,
    lsem, vss, vrs, yss, yrs, fss, frs, ess, ers, hss, hrs,
):
    rows, cols, nz, nx, ny, nv, wall_norm, wall, norm = cfg
    cells = rows * cols
    cc = CHUNK * cols
    nch = rows // CHUNK
    nb = 2 * nz
    gx, gy, vt = lax.axis_index("gx"), lax.axis_index("gy"), lax.axis_index("vert")
    right, left = {"gx": lax.rem(gx + 1, nx)}, {"gx": lax.rem(gx + nx - 1, nx)}
    above, below = {"gy": lax.rem(gy + 1, ny)}, {"gy": lax.rem(gy + ny - 1, ny)}
    peers = [{"vert": lax.rem(vt + k, nv)} for k in range(1, nv)]
    everyone = [right, left] + ([above] if ny == 2 else [above, below]) + peers

    def order(p):
        odd, half = lax.rem(p, 2), lax.div(p, 2)
        return (1 - odd) * half + odd * (nch - 1 - half)

    def span(k, size=cc, base=0):
        return pl.ds(pl.multiple_of(k * cc + base, LANES), size)

    def block(b):
        return (b % 2) * nz + b // 2

    def local_copies(k):
        return [
            pltpu.make_async_copy(
                f_hbm.at[pl.ds(k * CHUNK, CHUNK), :, pl.ds(b * LANES, LANES)],
                fa.at[pl.ds(1 + k * CHUNK, CHUNK), block(b), pl.ds(PAD, cols), :],
                lsem.at[k, b],
            )
            for b in range(nb)
        ]

    for p in range(nch):
        for c in local_copies(p // 2 if p % 2 == 0 else nch - 1 - p // 2):
            c.start()

    for s in range(STEPS):
        q[s, :, 0:LANES] = jnp.zeros((40, LANES), F32)
        q[s, :, LANES + cells : 2 * LANES + cells] = jnp.zeros((40, LANES), F32)

    barrier = pltpu.get_barrier_semaphore()
    for dev in everyone:
        pl.semaphore_signal(barrier, inc=1, device_id=dev, device_id_type=MESH)

    def remote(src, dst, ss, rs, dev):
        return pltpu.make_async_remote_copy(
            src_ref=src, dst_ref=dst, send_sem=ss, recv_sem=rs, device_id=dev, device_id_type=MESH
        )

    def q_cols(s, k):
        at = span(k, cc, LANES)
        return [
            remote(q.at[s, pl.ds(24, 8), at], qy.at[s, 0, :, span(k)], yss.at[s, k, 0], yrs.at[s, k, 0], above),
            remote(q.at[s, pl.ds(32, 8), at], qy.at[s, 1, :, span(k)], yss.at[s, k, 1], yrs.at[s, k, 1], below),
        ]

    def q_first_row(s):
        return remote(q.at[s, pl.ds(16, 8), pl.ds(LANES, LANES)],
                      q.at[s, pl.ds(16, 8), pl.ds(LANES + cells, LANES)], ess.at[s, 0], ers.at[s, 0], left)

    def q_last_row(s):
        return remote(q.at[s, pl.ds(8, 8), pl.ds(cells, LANES)],
                      q.at[s, pl.ds(8, 8), pl.ds(0, LANES)], ess.at[s, 1], ers.at[s, 1], right)

    def f_cols(s, buf, k):
        at = pl.ds(1 + k * CHUNK, CHUNK)
        return [
            remote(buf.at[at, :, pl.ds(PAD + cols - 1, 1), :], buf.at[at, :, pl.ds(PAD - 1, 1), :],
                   fss.at[s, k, 0], frs.at[s, k, 0], above),
            remote(buf.at[at, :, pl.ds(PAD, 1), :], buf.at[at, :, pl.ds(PAD + cols, 1), :],
                   fss.at[s, k, 1], frs.at[s, k, 1], below),
        ]

    def f_first_row(s, buf):
        return remote(buf.at[1, pl.ds(0, nz), pl.ds(PAD, cols), :],
                      buf.at[rows + 1, pl.ds(0, nz), pl.ds(PAD, cols), :], hss.at[s, 0], hrs.at[s, 0], left)

    def f_last_row(s, buf):
        return remote(buf.at[rows, pl.ds(nz, nz), pl.ds(PAD, cols), :],
                      buf.at[0, pl.ds(nz, nz), pl.ds(PAD, cols), :], hss.at[s, 1], hrs.at[s, 1], right)

    def z_copies(s, k):
        return [
            remote(a_ref.at[s, pl.ds(0, 6), span(k)], r_ref.at[s, j, pl.ds(0, 6), span(k)],
                   vss.at[s, k, j], vrs.at[s, k, j], peers[j])
            for j in range(nv - 1)
        ]

    z0 = (vt.astype(F32) * nz + (nz - 1) / 2.0 - (NVEL - 1) / 2.0) * H
    vz = [z0 + (z - (nz - 1) / 2.0) * H for z in range(nz)]
    for z in range(nz):
        szr[z] = jnp.exp(jnp.full((8, LANES), 0.0, F32) - vz[z] * vz[z] / (2 * WALL_T))
    wold[...] = jnp.zeros_like(wold)

    code = jnp.where(sol[...] == 1, nor[...] + 1, 0).astype(F32).astype(BF16)
    row_of = lax.broadcasted_iota(jnp.int32, (rows, cells), 0) * cols
    lane_of = lax.broadcasted_iota(jnp.int32, (rows, cells), 1)
    pick_row = jnp.where((lane_of >= row_of) & (lane_of < row_of + cols), 1.0, 0.0).astype(BF16)
    spread_code = lax.dot_general(code, pick_row, (((1,), (0,)), ((), ())), preferred_element_type=F32)
    col_lane = lax.broadcasted_iota(jnp.int32, (cols, cells), 1) % cols
    col_of = lax.broadcasted_iota(jnp.int32, (cols, cells), 0)
    code = jnp.sum(jnp.where(col_lane == col_of, spread_code, 0.0), axis=0, keepdims=True)
    flat = lax.broadcasted_iota(jnp.int32, (1, cells), 1) % cols
    outside = lax.broadcasted_iota(jnp.int32, (8, cells + 2 * LANES), 0)
    masks[...] = jnp.where(outside == 0, 1.0, 0.0)
    kinds = [code < 0.5] + [jnp.abs(code - (k + 1)) < 0.5 for k in range(4)]
    kinds += [code > 0.5, flat == 0, flat == cols - 1]
    for n, on in enumerate(kinds):
        masks[n : n + 1, LANES : LANES + cells] = jnp.where(on, 1.0, 0.0)

    def moments(s, k):
        dims = (((1,), (1,)), ((), ()))
        o = lax.dot_general(w_ref[...], halves[0], dims, preferred_element_type=F32)
        o = o + lax.dot_general(w_ref[...], halves[1], dims, preferred_element_type=F32)
        q[s, :, span(k, cc, LANES)] = o

    def keep_halves(r, b, tiles):
        new = jnp.concatenate(tiles, axis=0)
        hi = new.astype(BF16)
        at = slice(r * cols, (r + 1) * cols)
        ln = slice(b * LANES, (b + 1) * LANES)
        halves[0, at, ln] = hi
        halves[1, at, ln] = (new - hi.astype(F32)).astype(BF16)

    def send(s, buf, p, k):
        for c in q_cols(s, k) + f_cols(s, buf, k):
            c.start()

        @pl.when(p == 0)
        def _():
            q_first_row(s).start()
            f_first_row(s, buf).start()

        @pl.when(p == 1)
        def _():
            q_last_row(s).start()
            f_last_row(s, buf).start()

    def part(j):
        s, p = lax.div(j, nch), lax.rem(j, nch)
        k = order(p)
        for c in q_cols(s, k):
            c.wait()

        @pl.when(p == 0)
        def _():
            q_last_row(s).wait()

        @pl.when(p == 1)
        def _():
            q_first_row(s).wait()

        wide = span(k, cc + 2 * LANES)
        mid = slice(LANES, LANES + cc)

        def roll(v, by):
            return pltpu.roll(v, by % v.shape[1], 1)

        gas_w = masks[0:1, wide]
        xpw, xmw = q[s, 8:16, wide], q[s, 16:24, wide]
        ypw, ymw = q[s, 24:32, wide], q[s, 32:40, wide]

        def pick(n, v):
            return jnp.where(masks[n : n + 1, wide] > 0.5, v, 0.0)

        inc = (pick(1, roll(xmw[0:1], -cols)) + pick(2, roll(xpw[0:1], cols))
               + pick(3, roll(ymw[0:1], -1)) + pick(4, roll(ypw[0:1], 1))) * (H / 2)
        gas = masks[0:1, span(k, cc, LANES)]
        first_col = masks[6:7, span(k, cc, LANES)] > 0.5
        last_col = masks[7:8, span(k, cc, LANES)] > 0.5
        solid = masks[5:6, span(k, cc, LANES)] > 0.5
        xp, xm, yp, ym = (v[:, mid] for v in (xpw, xmw, ypw, ymw))
        base = (q[s, 0:8, span(k, cc, LANES)] - (COURANT * H / 2) * (xp + xm + yp + ym)) * gas
        sxp, sxm = roll(xpw * gas_w, cols)[:, mid], roll(xmw * gas_w, -cols)[:, mid]
        syp = jnp.where(first_col, roll(qy[s, 0, :, span(k)], 1 - cols), roll(yp * gas, 1))
        sym = jnp.where(last_col, roll(qy[s, 1, :, span(k)], cols - 1), roll(ym * gas, -1))
        a = base + (COURANT * H / 2) * (sxp + sxm + syp + sym)
        rho, mz = a[0:1], (H / 2) * a[3:4]
        e = (H * H / 4) * (8.0 * (a[4:5] + a[5:6]) + 3.0 * rho)
        lane = lax.broadcasted_iota(jnp.int32, (1, cc), 1)
        near = jnp.where(lane < cols, roll(inc, cols)[:, mid], roll(inc, -cols)[:, mid])
        lines = [jnp.where(solid, inc[:, mid], rho), (H / 2) * a[1:2], (H / 2) * a[2:3],
                 mz + z0 * rho, e + 2 * z0 * mz + z0 * z0 * rho, near]
        for r, line in enumerate(lines):
            a_ref[s, r : r + 1, span(k)] = line
        for c in z_copies(s, k):
            c.start()

    def params(s, k):
        for c in z_copies(s, k):
            c.wait()
        tot = a_ref[s, :, span(k)]
        for j in range(nv - 1):
            tot = tot + r_ref[s, j, :, span(k)]
        p_ref[0:8, :] = tot
        solid = masks[5:6, span(k, cc, LANES)] > 0.5
        lane = lax.broadcasted_iota(jnp.int32, (1, cc), 1)
        w = jnp.where(solid, p_ref[0:1, :] * (1.0 / wall_norm), 0.0)
        edge = p_ref[5:6, :] * (1.0 / wall_norm)

        def around(v, ve):
            return [jnp.where(lane < cols, ve, pltpu.roll(v, cols, 1)),
                    jnp.where(lane >= cc - cols, ve, pltpu.roll(v, cc - cols, 1)),
                    pltpu.roll(v, 1, 1), pltpu.roll(v, cc - 1, 1)]

        near = around(w, edge)
        dnear = around(w - wold[0:1, span(k)], edge - wold[1:2, span(k)])
        wold[0:1, span(k)] = w
        wold[1:2, span(k)] = edge
        mom = []
        for r in range(5):
            m = p_ref[r : r + 1, :]
            for d in range(4):
                if abs(wall[r][d]) > 1e-12 * abs(wall[0][0]):
                    m = m + wall[r][d] * near[d]
            mom.append(m)
        rho = mom[0]
        over = 1.0 / rho
        ux, uy, uz = mom[1] * over, mom[2] * over, mom[3] * over
        temp = (mom[4] * over - (ux * ux + uy * uy + uz * uz)) / 3.0
        rate = (INV_TAU / NVEL**3) * rho * jnp.exp(0.28 * jnp.log(temp))
        two_pi_t = (2.0 * math.pi) * temp
        inv = 1.0 / (1.0 + rate)
        amp = rate * inv * rho * H**3 / (two_pi_t * jnp.sqrt(two_pi_t))
        ux, uy, uz = (jnp.where(solid, 0.0, v) for v in (ux, uy, uz))
        g = jnp.where(solid, 0.5 / WALL_T, 0.5 / temp)
        amp = jnp.where(solid, w * norm, amp)
        inv = jnp.where(solid, 0.0, inv)
        g2 = g * math.log2(math.e)
        lines = [-g2 * (ux * ux + uy * uy), 2 * g2 * ux, 2 * g2 * uy, -g2]
        lines += [amp * jnp.exp(-g * (vz[z] - uz) * (vz[z] - uz)) for z in range(nz)]
        lines += [inv] + [inv * d for d in dnear]
        lines += [jnp.zeros_like(inv)] * (16 - len(lines))
        for r in range(16):
            p_ref[r : r + 1, :] = lines[r]
        pv = p_ref[...]
        ph = pv.astype(BF16)
        rest = pv - ph.astype(F32)
        pm = rest.astype(BF16)
        plo = (rest - pm.astype(F32)).astype(BF16)
        for n, piece in enumerate([ph, ph, pm, ph, pm, plo]):
            pst[16 * n : 16 * n + 16, :] = piece
        bc[...] = lax.dot_general(pst[...], b_ref[...], (((0,), (0,)), ((), ())), preferred_element_type=F32)

    def load(k):
        for c in local_copies(k):
            c.wait()
        ones = (lax.broadcasted_iota(jnp.int32, (8, LANES), 0) == 0).astype(BF16)
        bc[:, 0:LANES] = lax.dot_general(masks[0:8, span(k, cc, LANES)].astype(BF16), ones,
                                         (((0,), (0,)), ((), ())), preferred_element_type=F32)
        for r in range(CHUNK):
            i = 1 + k * CHUNK + r
            for b in range(nb):
                tiles = []
                for t in range(cols // 8):
                    at = slice(PAD + 8 * t, PAD + 8 * t + 8)
                    v = fa[i, block(b), at, :]
                    fa[i, block(b), at, :] = v * bc[r * cols + 8 * t : r * cols + 8 * t + 8, 0:LANES]
                    tiles.append(v)
                keep_halves(r, b, tiles)

    def relax(k, src, dst):
        up = vec[4] > 0.5
        for r in range(CHUNK):
            i = k * CHUNK + r
            for half in range(2):
                for t in range(cols // 8):
                    at = slice(r * cols + 8 * t, r * cols + 8 * t + 8)

                    def take(n):
                        return bc[at, n * LANES : (n + 1) * LANES]

                    bc[at, half * LANES : (half + 1) * LANES] = jnp.exp2(take(half))
                for z in range(nz):
                    b = 2 * z + half
                    tiles = []
                    for t in range(cols // 8):
                        at = slice(r * cols + 8 * t, r * cols + 8 * t + 8)

                        def take(n):
                            return bc[at, n * LANES : (n + 1) * LANES]

                        c0 = PAD + 8 * t
                        here = src[1 + i, block(b), c0 : c0 + 8, :]
                        side = src[i if half == 1 else i + 2, block(b), c0 : c0 + 8, :]
                        s = jnp.where(up, src[1 + i, block(b), c0 - 1 : c0 + 7, :],
                                      src[1 + i, block(b), c0 + 1 : c0 + 9, :])
                        moved = here * vec[half] + side * vec[2 + half] + s
                        new = moved * take(2 + nz) + (take(3 + nz + half) * szr[z] + take(2 + z) * take(half))
                        if dst is None:
                            out[i, 8 * t : 8 * t + 8, b * LANES : (b + 1) * LANES] = new
                        else:
                            dst[1 + i, block(b), c0 : c0 + 8, :] = new
                            tiles.append(new)
                    if dst is not None:
                        keep_halves(r, b, tiles)

    pl.semaphore_wait(barrier, len(everyone))

    def stage_load(p, carry):
        k = order(p)
        load(k)
        moments(0, k)
        send(0, fa, p, k)

        @pl.when(p >= LAG)
        def _():
            part(p - LAG)

        return carry

    lax.fori_loop(0, nch, stage_load, 0)

    for step in range(1, STEPS + 1):
        src = fa if step % 2 == 1 else fb
        dst = None if step == STEPS else (fb if step % 2 == 1 else fa)

        def stage(p, carry, step=step, src=src, dst=dst):
            k = order(p)
            for c in f_cols(step - 1, src, k):
                c.wait()

            @pl.when(p == 0)
            def _():
                f_last_row(step - 1, src).wait()

            @pl.when(p == 1)
            def _():
                f_first_row(step - 1, src).wait()

            params(step - 1, k)
            relax(k, src, dst)
            if dst is not None:
                moments(step, k)
                send(step, dst, p, k)
                part(step * nch + p - LAG)
            else:

                @pl.when(p < LAG)
                def _():
                    part(step * nch + p - LAG)

            return carry

        lax.fori_loop(0, nch, stage, 0)


def solution(mesh):
    nx, ny, nv = mesh.shape["gx"], mesh.shape["gy"], mesh.shape["vert"]

    def on_device(f, solid_mask, normal_code):
        rows, cols, vel = f.shape
        nz = vel // PLANE
        cells = rows * cols
        w, bst, vec, wall_norm, wall, norm = tables(nz)
        nch = rows // CHUNK
        cfg = (rows, cols, nz, nx, ny, nv, wall_norm, wall, norm)
        vm = pl.BlockSpec(memory_space=pltpu.VMEM)
        dma = pltpu.SemaphoreType.DMA
        bw = bst.shape[1]
        cc = CHUNK * cols
        field = (rows + 2, 2 * nz, cols + SLOTS, LANES)
        return pl.pallas_call(
            functools.partial(kernel, cfg),
            out_shape=pltpu.VMEM((rows, cols, vel), F32),
            in_specs=[pl.BlockSpec(memory_space=pl.ANY), vm, vm, vm, vm, vm],
            out_specs=vm,
            scratch_shapes=[
                pltpu.VMEM(field, F32),
                pltpu.VMEM(field, F32),
                pltpu.VMEM((cc, bw), F32),
                pltpu.VMEM((STEPS, 40, cells + 2 * LANES), F32),
                pltpu.VMEM((STEPS, 2, 8, cells), F32),
                pltpu.VMEM((STEPS, 8, cells), F32),
                pltpu.VMEM((STEPS, nv - 1, 8, cells), F32),
                pltpu.VMEM((16, cc), F32),
                pltpu.VMEM((96, cc), BF16),
                pltpu.VMEM((2, cc, vel), BF16),
                pltpu.VMEM((8, cells), F32),
                pltpu.VMEM((8, cells + 2 * LANES), F32),
                pltpu.VMEM((nz, 8, LANES), F32),
                dma((nch, 2 * nz)),
                dma((STEPS, nch, nv - 1)), dma((STEPS, nch, nv - 1)),
                dma((STEPS, nch, 2)), dma((STEPS, nch, 2)),
                dma((STEPS, nch, 2)), dma((STEPS, nch, 2)),
                dma((STEPS, 2)), dma((STEPS, 2)),
                dma((STEPS, 2)), dma((STEPS, 2)),
            ],
            compiler_params=pltpu.CompilerParams(
                collective_id=0, has_side_effects=True, vmem_limit_bytes=46 * 2**20
            ),
        )(f, solid_mask.T, normal_code.T, jnp.asarray(w), jnp.asarray(bst), jnp.asarray(vec))

    placed = (P("gx", "gy", "vert"), P("gx", "gy"), P("gx", "gy"))
    return jax.shard_map(
        on_device, mesh=mesh, in_specs=placed, out_specs=P("gx", "gy", "vert"), check_vma=False
    )
```

time: 71.7 us -> 56.5 us (0.79)
  Pallas kernels: 69.8 us -> 53 us
  local copies, waits for them, and re-layouts: 0.77 us -> 3.4 us
  other arithmetic: 0.74 us -> 0 us
    pallas_call x2 -> x1, Pallas kernels: 69.8 us -> 53 us  [on_device(): pl.pallas_call(functools.partial(kernel, cfg), out_shape=pltpu.VMEM((rows...]
    unnamed x0 -> x1, local copies, waits for them, and re-layouts: none -> 3.4 us
    select_n x1 -> x0, other arithmetic: 0.74 us -> none  [on_device(): code = jnp.where(solid_mask == 1, normal_code + 1, 0).reshape(1, cells)]
where the time goes in v1:
time: 56.5 us; the launch traced here: 56.4 us
  Pallas kernels  53 us (94%)
  local copies, waits for them, and re-layouts  3.4 us (6%)
    pallas_call x1, Pallas kernels, on_device(): pl.pallas_call(functools.partial(kernel, cfg), out_shape=pltpu.VMEM((rows...  53 us
    unnamed x1, local copies, waits for them, and re-layouts  3.4 us

profile of v1, /device:TPU:0, one launch (start us, length us, event | category | flops | bytes accessed | tf_op | source)
XLA Modules:
  0.0 56.4 jit_solution(17393511136018352914)
XLA Ops:
  0.0 53.0 %shard_map.64 = f32[64,32,1024]{2,1,0:T(8,128)S(1)} custom-call(f32[64,32,1024]{2,1,0:T(8,128)} %f_hbm.1, s32[32,64]{1,0:T(8,128)} %bitcast.2, s32[32,64]{1,0:T(8,128)} %bitcast.3, bf16[40,1024]{1,0:T(8,128)(2,1)} %constant.6.clone.w_ref, bf16[96,1152]{1,0:T(8,128)(2,1)} %constant.7.clone.b_ref, f32[5,8,128]{2,1,0:T(8,128)} %constant.8.clone.vec), custom_call_target="tpu_custom_call" | custom-call | tf_op jit(solution)/shard_map/pallas_call | solution.py:469
  53.0 3.4 %copy.8 = f32[64,32,1024]{2,1,0:T(8,128)} copy(f32[64,32,1024]{2,1,0:T(8,128)S(1)} %shard_map.64) | data formatting | bytes 16777216

commit v2 on v1

--- a/solution.py
+++ b/solution.py
@@ -23,7 +23,7 @@
 F32 = jnp.float32
 BF16 = jnp.bfloat16
 CHUNK = 8
-LAG = 2
+LAG = 3
 PAD = 8
 SLOTS = 16
 
@@ -102,7 +102,7 @@
 
 def kernel(
     cfg, f_hbm, sol, nor, w_ref, b_ref, vec, out,
-    fa, fb, bc, q, qy, a_ref, r_ref, p_ref, pst, halves, wold, masks, szr,
+    fa, fb, bca, bcb, q, qy, a_ref, r_ref, x_ref, xr_ref, p_ref, pst, halfa, halfb, acc, wold, masks, szr,
     lsem, vss, vrs, yss, yrs, fss, frs, ess, ers, hss, hrs,
 ):
     rows, cols, nz, nx, ny, nv, wall_norm, wall, norm = cfg
@@ -114,11 +114,25 @@
     right, left = {"gx": lax.rem(gx + 1, nx)}, {"gx": lax.rem(gx + nx - 1, nx)}
     above, below = {"gy": lax.rem(gy + 1, ny)}, {"gy": lax.rem(gy + ny - 1, ny)}
     peers = [{"vert": lax.rem(vt + k, nv)} for k in range(1, nv)]
-    everyone = [right, left] + ([above] if ny == 2 else [above, below]) + peers
-
-    def order(p):
-        odd, half = lax.rem(p, 2), lax.div(p, 2)
-        return (1 - odd) * half + odd * (nch - 1 - half)
+    lefts = [left] + [{**left, **p} for p in peers]
+    rights = [right] + [{**right, **p} for p in peers]
+    everyone = lefts + rights + ([above] if ny == 2 else [above, below]) + peers
+
+    pairs = nch // 2
+    bcs, halfs = [bca, bcb], [halfa, halfb]
+
+    def chunk_at(m, e):
+        return m if e == 0 else nch - 1 - m
+
+    def before(step, m, e):
+        if e == 1:
+            return step, m, 0
+        return step - 1 + lax.div(m + pairs - 1, pairs), lax.rem(m + pairs - 1, pairs), 1
+
+    def after(step, m, e):
+        if e == 0:
+            return step, m, 1
+        return step + lax.div(m + 1, pairs), lax.rem(m + 1, pairs), 0
 
     def span(k, size=cc, base=0):
         return pl.ds(pl.multiple_of(k * cc + base, LANES), size)
@@ -160,13 +174,11 @@
             remote(q.at[s, pl.ds(32, 8), at], qy.at[s, 1, :, span(k)], yss.at[s, k, 1], yrs.at[s, k, 1], below),
         ]
 
-    def q_first_row(s):
-        return remote(q.at[s, pl.ds(16, 8), pl.ds(LANES, LANES)],
-                      q.at[s, pl.ds(16, 8), pl.ds(LANES + cells, LANES)], ess.at[s, 0], ers.at[s, 0], left)
-
-    def q_last_row(s):
-        return remote(q.at[s, pl.ds(8, 8), pl.ds(cells, LANES)],
-                      q.at[s, pl.ds(8, 8), pl.ds(0, LANES)], ess.at[s, 1], ers.at[s, 1], right)
+    def edge_copies(s, e):
+        return [
+            remote(x_ref.at[s, e], xr_ref.at[s, e, j], ess.at[s, e, j], ers.at[s, e, j], dev)
+            for j, dev in enumerate(lefts if e == 0 else rights)
+        ]
 
     def f_cols(s, buf, k):
         at = pl.ds(1 + k * CHUNK, CHUNK)
@@ -214,13 +226,22 @@
     for n, on in enumerate(kinds):
         masks[n : n + 1, LANES : LANES + cells] = jnp.where(on, 1.0, 0.0)
 
-    def moments(s, k):
-        dims = (((1,), (1,)), ((), ()))
-        o = lax.dot_general(w_ref[...], halves[0], dims, preferred_element_type=F32)
-        o = o + lax.dot_general(w_ref[...], halves[1], dims, preferred_element_type=F32)
-        q[s, :, span(k, cc, LANES)] = o
-
-    def keep_halves(r, b, tiles):
+    def moments_piece(s, k, halves, n):
+        ln = slice(n // 2 * PLANE, (n // 2 + 1) * PLANE)
+        o = lax.dot_general(w_ref[:, ln], halves[n % 2, :, ln], (((1,), (1,)), ((), ())),
+                            preferred_element_type=F32)
+        if n > 0:
+            o = o + acc[...]
+        if n < nb - 1:
+            acc[...] = o
+        else:
+            q[s, :, span(k, cc, LANES)] = o
+
+    def moments(s, k, halves):
+        for n in range(nb):
+            moments_piece(s, k, halves, n)
+
+    def keep_halves(halves, r, b, tiles):
         new = jnp.concatenate(tiles, axis=0)
         hi = new.astype(BF16)
         at = slice(r * cols, (r + 1) * cols)
@@ -228,33 +249,52 @@
         halves[0, at, ln] = hi
         halves[1, at, ln] = (new - hi.astype(F32)).astype(BF16)
 
-    def send(s, buf, p, k):
-        for c in q_cols(s, k) + f_cols(s, buf, k):
+    def send_f(s, buf, m, e):
+        for c in f_cols(s, buf, chunk_at(m, e)):
             c.start()
 
-        @pl.when(p == 0)
+        @pl.when(m == 1)
         def _():
-            q_first_row(s).start()
-            f_first_row(s, buf).start()
-
-        @pl.when(p == 1)
+            (f_last_row if e else f_first_row)(s, buf).start()
+
+    def wait_f(s, buf, m, e):
+        for c in f_cols(s, buf, chunk_at(m, e)):
+            c.wait()
+
+        @pl.when(m == 0)
         def _():
-            q_last_row(s).start()
-            f_last_row(s, buf).start()
-
-    def part(j):
-        s, p = lax.div(j, nch), lax.rem(j, nch)
-        k = order(p)
+            (f_first_row if e else f_last_row)(s, buf).wait()
+
+    def physical(a):
+        rho, mz = a[0:1], (H / 2) * a[3:4]
+        e = (H * H / 4) * (8.0 * (a[4:5] + a[5:6]) + 3.0 * rho)
+        return [rho, (H / 2) * a[1:2], (H / 2) * a[2:3], mz + z0 * rho, e + 2 * z0 * mz + z0 * z0 * rho]
+
+    def send_q(s, m, e):
+        for c in q_cols(s, chunk_at(m, e)):
+            c.start()
+
+        @pl.when(m == 0)
+        def _():
+            if e == 0:
+                a = q[s, 16:24, LANES : 2 * LANES]
+                a = pltpu.roll(a, LANES - cols, 1)
+                here = lax.broadcasted_iota(jnp.int32, (8, LANES), 1) >= LANES - cols
+            else:
+                a = q[s, 8:16, cells : cells + LANES]
+                a = pltpu.roll(a, cols, 1)
+                here = lax.broadcasted_iota(jnp.int32, (8, LANES), 1) < cols
+            a = jnp.where(here, a * (COURANT * H / 2), 0.0)
+            for r, line in enumerate(physical(a)):
+                x_ref[s, e, r : r + 1] = line
+            x_ref[s, e, 5:8] = jnp.zeros((3, LANES), F32)
+            for c in edge_copies(s, e):
+                c.start()
+
+    def part(s, m, e):
+        k = chunk_at(m, e)
         for c in q_cols(s, k):
             c.wait()
-
-        @pl.when(p == 0)
-        def _():
-            q_last_row(s).wait()
-
-        @pl.when(p == 1)
-        def _():
-            q_first_row(s).wait()
 
         wide = span(k, cc + 2 * LANES)
         mid = slice(LANES, LANES + cc)
@@ -281,20 +321,16 @@
         syp = jnp.where(first_col, roll(qy[s, 0, :, span(k)], 1 - cols), roll(yp * gas, 1))
         sym = jnp.where(last_col, roll(qy[s, 1, :, span(k)], cols - 1), roll(ym * gas, -1))
         a = base + (COURANT * H / 2) * (sxp + sxm + syp + sym)
-        rho, mz = a[0:1], (H / 2) * a[3:4]
-        e = (H * H / 4) * (8.0 * (a[4:5] + a[5:6]) + 3.0 * rho)
+        lines = physical(a)
         lane = lax.broadcasted_iota(jnp.int32, (1, cc), 1)
         near = jnp.where(lane < cols, roll(inc, cols)[:, mid], roll(inc, -cols)[:, mid])
-        lines = [jnp.where(solid, inc[:, mid], rho), (H / 2) * a[1:2], (H / 2) * a[2:3],
-                 mz + z0 * rho, e + 2 * z0 * mz + z0 * z0 * rho, near]
+        lines = [jnp.where(solid, inc[:, mid], lines[0])] + lines[1:] + [near]
         for r, line in enumerate(lines):
             a_ref[s, r : r + 1, span(k)] = line
         for c in z_copies(s, k):
             c.start()
 
     def params(s, k):
-        for c in z_copies(s, k):
-            c.wait()
         tot = a_ref[s, :, span(k)]
         for j in range(nv - 1):
             tot = tot + r_ref[s, j, :, span(k)]
@@ -346,11 +382,14 @@
         plo = (rest - pm.astype(F32)).astype(BF16)
         for n, piece in enumerate([ph, ph, pm, ph, pm, plo]):
             pst[16 * n : 16 * n + 16, :] = piece
-        bc[...] = lax.dot_general(pst[...], b_ref[...], (((0,), (0,)), ((), ())), preferred_element_type=F32)
-
-    def load(k):
-        for c in local_copies(k):
-            c.wait()
+
+    def spread_piece(bc, n):
+        ln = slice(n * PLANE, min((n + 1) * PLANE, bc.shape[1]))
+        bc[:, ln] = lax.dot_general(pst[...], b_ref[:, ln], (((0,), (0,)), ((), ())), preferred_element_type=F32)
+
+    spreads = -(-bca.shape[1] // PLANE)
+
+    def load(k, bc, halves):
         ones = (lax.broadcasted_iota(jnp.int32, (8, LANES), 0) == 0).astype(BF16)
         bc[:, 0:LANES] = lax.dot_general(masks[0:8, span(k, cc, LANES)].astype(BF16), ones,
                                          (((0,), (0,)), ((), ())), preferred_element_type=F32)
@@ -363,11 +402,12 @@
                     v = fa[i, block(b), at, :]
                     fa[i, block(b), at, :] = v * bc[r * cols + 8 * t : r * cols + 8 * t + 8, 0:LANES]
                     tiles.append(v)
-                keep_halves(r, b, tiles)
-
-    def relax(k, src, dst):
+                keep_halves(halves, r, b, tiles)
+
+    def relax(k, src, dst, bc, halves, beside):
         up = vec[4] > 0.5
         for r in range(CHUNK):
+            beside(r)
             i = k * CHUNK + r
             for half in range(2):
                 for t in range(cols // 8):
@@ -399,56 +439,106 @@
                             dst[1 + i, block(b), c0 : c0 + 8, :] = new
                             tiles.append(new)
                     if dst is not None:
-                        keep_halves(r, b, tiles)
+                        keep_halves(halves, r, b, tiles)
 
     pl.semaphore_wait(barrier, len(everyone))
 
-    def stage_load(p, carry):
-        k = order(p)
-        load(k)
-        moments(0, k)
-        send(0, fa, p, k)
-
-        @pl.when(p >= LAG)
+    def stage_load(m, first):
+        for e in range(2):
+            for c in local_copies(chunk_at(m, e)):
+                c.wait()
+        if not first:
+            moments(0, chunk_at(m - 1, 1), halfb)
+        load(chunk_at(m, 0), bca, halfa)
+        moments(0, chunk_at(m, 0), halfa)
+        load(chunk_at(m, 1), bcb, halfb)
+        if not first:
+            send_q(0, m - 1, 1)
+        send_q(0, m, 0)
+        for e in range(2):
+            send_f(0, fa, m, e)
+        if not first:
+
+            @pl.when(m > 1)
+            def _():
+                part(0, m - 2, 1)
+
+            part(0, m - 1, 0)
+
+    stage_load(0, True)
+
+    def load_more(m, carry):
+        stage_load(m, False)
+        return carry
+
+    lax.fori_loop(1, pairs, load_more, 0)
+
+    def wait_z(s, m, e):
+        k = chunk_at(m, e)
+        for c in z_copies(s, k):
+            c.wait()
+
+        @pl.when(m == 0)
         def _():
-            part(p - LAG)
-
-        return carry
-
-    lax.fori_loop(0, nch, stage_load, 0)
+            for c in edge_copies(s, 1 - e):
+                c.wait()
+            at = span(k, LANES, e * (cc - LANES))
+            total = a_ref[s, :, at]
+            for j in range(nv):
+                total = total + xr_ref[s, 1 - e, j]
+            a_ref[s, :, at] = total
 
     for step in range(1, STEPS + 1):
         src = fa if step % 2 == 1 else fb
         dst = None if step == STEPS else (fb if step % 2 == 1 else fa)
 
-        def stage(p, carry, step=step, src=src, dst=dst):
-            k = order(p)
-            for c in f_cols(step - 1, src, k):
-                c.wait()
-
-            @pl.when(p == 0)
-            def _():
-                f_last_row(step - 1, src).wait()
-
-            @pl.when(p == 1)
-            def _():
-                f_first_row(step - 1, src).wait()
-
-            params(step - 1, k)
-            relax(k, src, dst)
-            if dst is not None:
-                moments(step, k)
-                send(step, dst, p, k)
-                part(step * nch + p - LAG)
-            else:
-
-                @pl.when(p < LAG)
-                def _():
-                    part(step * nch + p - LAG)
-
+        def stage(m, ending, step=step, src=src, dst=dst):
+            for e in range(2):
+                k = chunk_at(m, e)
+                sn, mn, en = after(step - 1, m, e)
+                sp, mp, ep = before(step, m, e)
+                done = ending and e == 1
+                wait_f(step - 1, src, m, e)
+                if not done:
+                    wait_z(sn, mn, en)
+                    params(sn, chunk_at(mn, en))
+
+                def beside(r):
+                    if dst is not None:
+                        for n in range(nb):
+                            if n * CHUNK // nb == r:
+                                moments_piece(sp, chunk_at(mp, ep), halfs[1 - e], n)
+                    if not done:
+                        for n in range(spreads):
+                            if CHUNK - spreads + n == r:
+                                spread_piece(bcs[1 - e], n)
+
+                relax(k, src, dst, bcs[e], halfs[e], beside)
+                if dst is not None:
+                    send_q(sp, mp, ep)
+                    send_f(step, dst, m, e)
+                    at = step * nch + 2 * m + e - LAG
+                    part(lax.div(at, nch), lax.div(lax.rem(at, nch), 2), 1 - e)
+
+        if step == 1:
+            wait_z(0, 0, 0)
+            params(0, 0)
+            for n in range(spreads):
+                spread_piece(bca, n)
+        if dst is None:
+            moments(step - 1, chunk_at(pairs - 1, 1), halfb)
+            send_q(step - 1, pairs - 1, 1)
+            part(step - 1, pairs - 2, 1)
+            part(step - 1, pairs - 1, 0)
+            part(step - 1, pairs - 1, 1)
+
+        def trip(m, carry, stage=stage):
+            stage(m, False)
             return carry
 
-        lax.fori_loop(0, nch, stage, 0)
+        lax.fori_loop(0, pairs - (1 if dst is None else 0), trip, 0)
+        if dst is None:
+            stage(pairs - 1, True)
 
 
 def solution(mesh):
@@ -475,13 +565,18 @@
                 pltpu.VMEM(field, F32),
                 pltpu.VMEM(field, F32),
                 pltpu.VMEM((cc, bw), F32),
+                pltpu.VMEM((cc, bw), F32),
                 pltpu.VMEM((STEPS, 40, cells + 2 * LANES), F32),
                 pltpu.VMEM((STEPS, 2, 8, cells), F32),
                 pltpu.VMEM((STEPS, 8, cells), F32),
                 pltpu.VMEM((STEPS, nv - 1, 8, cells), F32),
+                pltpu.VMEM((STEPS, 2, 8, LANES), F32),
+                pltpu.VMEM((STEPS, 2, nv, 8, LANES), F32),
                 pltpu.VMEM((16, cc), F32),
                 pltpu.VMEM((96, cc), BF16),
                 pltpu.VMEM((2, cc, vel), BF16),
+                pltpu.VMEM((2, cc, vel), BF16),
+                pltpu.VMEM((40, cc), F32),
                 pltpu.VMEM((8, cells), F32),
                 pltpu.VMEM((8, cells + 2 * LANES), F32),
                 pltpu.VMEM((nz, 8, LANES), F32),
@@ -489,7 +584,7 @@
                 dma((STEPS, nch, nv - 1)), dma((STEPS, nch, nv - 1)),
                 dma((STEPS, nch, 2)), dma((STEPS, nch, 2)),
                 dma((STEPS, nch, 2)), dma((STEPS, nch, 2)),
-                dma((STEPS, 2)), dma((STEPS, 2)),
+                dma((STEPS, 2, nv)), dma((STEPS, 2, nv)),
                 dma((STEPS, 2)), dma((STEPS, 2)),
             ],
             compiler_params=pltpu.CompilerParams(

time: 56.5 us -> 50.3 us (0.89)
  Pallas kernels: 53 us -> 46.8 us
    pallas_call x1, Pallas kernels: 53 us -> 46.8 us  [on_device(): pl.pallas_call(functools.partial(kernel, cfg), out_shape=pltpu.VMEM((rows...]
where the time goes in v2:
time: 50.3 us; the launch traced here: 50.2 us
  Pallas kernels  46.8 us (93%)
  local copies, waits for them, and re-layouts  3.4 us (7%)
    pallas_call x1, Pallas kernels, on_device(): pl.pallas_call(functools.partial(kernel, cfg), out_shape=pltpu.VMEM((rows...  46.8 us
    unnamed x1, local copies, waits for them, and re-layouts  3.4 us

profile of v2, /device:TPU:0, one launch (start us, length us, event | category | flops | bytes accessed | tf_op | source)
XLA Modules:
  0.0 50.2 jit_solution(9341812443383139954)
XLA Ops:
  0.0 46.8 %shard_map.64 = f32[64,32,1024]{2,1,0:T(8,128)S(1)} custom-call(f32[64,32,1024]{2,1,0:T(8,128)} %f_hbm.1, s32[32,64]{1,0:T(8,128)} %bitcast.2, s32[32,64]{1,0:T(8,128)} %bitcast.3, bf16[40,1024]{1,0:T(8,128)(2,1)} %constant.6.clone.w_ref, bf16[96,1152]{1,0:T(8,128)(2,1)} %constant.7.clone.b_ref, f32[5,8,128]{2,1,0:T(8,128)} %constant.8.clone.vec), custom_call_target="tpu_custom_call" | custom-call | tf_op jit(solution)/shard_map/pallas_call | solution.py:559
  46.8 3.4 %copy.8 = f32[64,32,1024]{2,1,0:T(8,128)} copy(f32[64,32,1024]{2,1,0:T(8,128)S(1)} %shard_map.64) | data formatting | bytes 16777216

commit v3 on v2

--- a/solution.py
+++ b/solution.py
@@ -145,10 +145,16 @@
             pltpu.make_async_copy(
                 f_hbm.at[pl.ds(k * CHUNK, CHUNK), :, pl.ds(b * LANES, LANES)],
                 fa.at[pl.ds(1 + k * CHUNK, CHUNK), block(b), pl.ds(PAD, cols), :],
-                lsem.at[k, b],
+                lsem.at[k],
             )
             for b in range(nb)
         ]
+
+    def both(ref, sem):
+        return pltpu.make_async_copy(ref, ref, sem)
+
+    def wait_local(k):
+        both(fa.at[pl.ds(1 + k * CHUNK, CHUNK), :, pl.ds(PAD, cols), :], lsem.at[k]).wait()
 
     for p in range(nch):
         for c in local_copies(p // 2 if p % 2 == 0 else nch - 1 - p // 2):
@@ -170,13 +176,13 @@
     def q_cols(s, k):
         at = span(k, cc, LANES)
         return [
-            remote(q.at[s, pl.ds(24, 8), at], qy.at[s, 0, :, span(k)], yss.at[s, k, 0], yrs.at[s, k, 0], above),
-            remote(q.at[s, pl.ds(32, 8), at], qy.at[s, 1, :, span(k)], yss.at[s, k, 1], yrs.at[s, k, 1], below),
+            remote(q.at[s, pl.ds(24, 8), at], qy.at[s, 0, :, span(k)], yss.at[s, k], yrs.at[s, k], above),
+            remote(q.at[s, pl.ds(32, 8), at], qy.at[s, 1, :, span(k)], yss.at[s, k], yrs.at[s, k], below),
         ]
 
     def edge_copies(s, e):
         return [
-            remote(x_ref.at[s, e], xr_ref.at[s, e, j], ess.at[s, e, j], ers.at[s, e, j], dev)
+            remote(x_ref.at[s, e], xr_ref.at[s, e, j], ess.at[s, e], ers.at[s, e], dev)
             for j, dev in enumerate(lefts if e == 0 else rights)
         ]
 
@@ -200,7 +206,7 @@
     def z_copies(s, k):
         return [
             remote(a_ref.at[s, pl.ds(0, 6), span(k)], r_ref.at[s, j, pl.ds(0, 6), span(k)],
-                   vss.at[s, k, j], vrs.at[s, k, j], peers[j])
+                   vss.at[s, k], vrs.at[s, k], peers[j])
             for j in range(nv - 1)
         ]
 
@@ -293,8 +299,8 @@
 
     def part(s, m, e):
         k = chunk_at(m, e)
-        for c in q_cols(s, k):
-            c.wait()
+        for sem in (yss, yrs):
+            both(qy.at[s, :, :, span(k)], sem.at[s, k]).wait()
 
         wide = span(k, cc + 2 * LANES)
         mid = slice(LANES, LANES + cc)
@@ -445,8 +451,7 @@
 
     def stage_load(m, first):
         for e in range(2):
-            for c in local_copies(chunk_at(m, e)):
-                c.wait()
+            wait_local(chunk_at(m, e))
         if not first:
             moments(0, chunk_at(m - 1, 1), halfb)
         load(chunk_at(m, 0), bca, halfa)
@@ -475,13 +480,13 @@
 
     def wait_z(s, m, e):
         k = chunk_at(m, e)
-        for c in z_copies(s, k):
-            c.wait()
+        for sem in (vss, vrs):
+            both(r_ref.at[s, :, pl.ds(0, 6), span(k)], sem.at[s, k]).wait()
 
         @pl.when(m == 0)
         def _():
-            for c in edge_copies(s, 1 - e):
-                c.wait()
+            for sem in (ess, ers):
+                both(xr_ref.at[s, 1 - e], sem.at[s, 1 - e]).wait()
             at = span(k, LANES, e * (cc - LANES))
             total = a_ref[s, :, at]
             for j in range(nv):
@@ -580,11 +585,11 @@
                 pltpu.VMEM((8, cells), F32),
                 pltpu.VMEM((8, cells + 2 * LANES), F32),
                 pltpu.VMEM((nz, 8, LANES), F32),
-                dma((nch, 2 * nz)),
-                dma((STEPS, nch, nv - 1)), dma((STEPS, nch, nv - 1)),
+                dma((nch,)),
+                dma((STEPS, nch)), dma((STEPS, nch)),
+                dma((STEPS, nch)), dma((STEPS, nch)),
                 dma((STEPS, nch, 2)), dma((STEPS, nch, 2)),
-                dma((STEPS, nch, 2)), dma((STEPS, nch, 2)),
-                dma((STEPS, 2, nv)), dma((STEPS, 2, nv)),
+                dma((STEPS, 2)), dma((STEPS, 2)),
                 dma((STEPS, 2)), dma((STEPS, 2)),
             ],
             compiler_params=pltpu.CompilerParams(

time: 50.3 us -> 47.8 us (0.950)
  Pallas kernels: 46.8 us -> 44.3 us
    pallas_call x1, Pallas kernels: 46.8 us -> 44.3 us  [on_device(): pl.pallas_call(functools.partial(kernel, cfg), out_shape=pltpu.VMEM((rows...]
where the time goes in v3:
time: 47.8 us; the launch traced here: 47.7 us
  Pallas kernels  44.3 us (93%)
  local copies, waits for them, and re-layouts  3.4 us (7%)
    pallas_call x1, Pallas kernels, on_device(): pl.pallas_call(functools.partial(kernel, cfg), out_shape=pltpu.VMEM((rows...  44.3 us
    unnamed x1, local copies, waits for them, and re-layouts  3.4 us

profile of v3, /device:TPU:0, one launch (start us, length us, event | category | flops | bytes accessed | tf_op | source)
XLA Modules:
  0.0 47.7 jit_solution(16516626462330135902)
XLA Ops:
  0.0 44.3 %shard_map.64 = f32[64,32,1024]{2,1,0:T(8,128)S(1)} custom-call(f32[64,32,1024]{2,1,0:T(8,128)} %f_hbm.1, s32[32,64]{1,0:T(8,128)} %bitcast.2, s32[32,64]{1,0:T(8,128)} %bitcast.3, bf16[40,1024]{1,0:T(8,128)(2,1)} %constant.6.clone.w_ref, bf16[96,1152]{1,0:T(8,128)(2,1)} %constant.7.clone.b_ref, f32[5,8,128]{2,1,0:T(8,128)} %constant.8.clone.vec), custom_call_target="tpu_custom_call" | custom-call | tf_op jit(solution)/shard_map/pallas_call | solution.py:564
  44.3 3.4 %copy.8 = f32[64,32,1024]{2,1,0:T(8,128)} copy(f32[64,32,1024]{2,1,0:T(8,128)S(1)} %shard_map.64) | data formatting | bytes 16777216
